TPU v7x, 32 devices: a whole 2x2x4 slice. The times are simulated.
32 devices in a mesh: groups: 2 (over y), rep: 4 (over x, core), tp: 4 (over z).
Axes of the slice: x: 2, y: 2, z: 4, core: 2. Of those that a mesh axis runs over, the one named last changes fastest.
Arguments:
- tokens: bfloat16 [3072, 8192], P(('groups', 'rep', 'tp')), parts along dimension 0, may hold values from -6 to 6
- base_weight: bfloat16 [8192, 2048], P(None, 'tp'), may hold values from -0.0625 to 0.0625
- delta_codes: bfloat16 [32768, 2048], P(('groups', 'rep'), 'tp'), parts along dimension 0, may hold values from -4 to 4
- delta_scales: bfloat16 [256, 16], P(('groups', 'rep'), 'tp'), parts along dimension 0, may hold values from 0.0019989014 to 0.011962891
- replica_variant: int32 [8], P('groups'), parts along dimension 0, may hold values from 0 to 1
- block_home: int32 [4, 64], P('groups'), parts along dimension 0, may hold values from 0 to 127, as said below
Outputs:
- key_value: bfloat16 [3072, 2048], P(('groups', 'rep'), 'tp'), parts along dimension 0
There are 2 independent parts, one for each index of `groups`. A program takes and returns all parts, laid end to end along the dimension named above; an argument that names none is the same for every part. Nothing has to cross between parts.
Inputs may be any that keep to these rules, and one draw needn't show every extreme that they name: `block_home`: the entries are a permutation of 0 to 127; entry e stands for slot e % 32 of holder e // 32, that is rows e * 128 to (e + 1) * 128 - 1 of delta_codes. At most 24 blocks of one variant lie with one holder, and in every draw some holders hold exactly 24 blocks of a variant.
All inputs are finite; a program needn't handle non-finite values.
Results may differ from a plain program's by a relative error of at most 0.0049.
Values may be sent and summed in bfloat16 or wider, within the bound.
A program may use at most 128 MiB of HBM per device.

v0:
```python
import jax
import jax.numpy as jnp
from jax import lax
from jax.sharding import PartitionSpec as P


def local(tokens, base_weight, delta_codes, delta_scales, replica_variant, block_home):
    holders = lax.axis_size("rep")
    holder_self = lax.axis_index("rep")
    variants = block_home.shape[0]
    blocks = block_home.shape[1]
    slots = blocks // 2
    capacity = 3 * blocks // (2 * holders)
    width = base_weight.shape[1]
    col_blocks = delta_scales.shape[1]
    block_size = width // col_blocks
    variant_hot = (
        replica_variant[:, None] == jnp.arange(variants, dtype=jnp.int32)[None, :]
    ).astype(jnp.int32)
    homes_each = jnp.sum(variant_hot[:, :, None] * block_home[None, :, :], axis=1)
    holder_each = homes_each // slots
    slot_each = homes_each % slots
    block_index = jnp.arange(blocks, dtype=jnp.int32)
    before = block_index[None, :] < block_index[:, None]
    same_holder = holder_each[:, :, None] == holder_each[:, None, :]
    rank_each = jnp.sum((same_holder & before[None, :, :]).astype(jnp.int32), axis=2)
    mine = holder_each == holder_self
    slot_index = jnp.arange(capacity, dtype=jnp.int32)
    picked = mine[:, None, :] & (rank_each[:, None, :] == slot_index[None, :, None])
    slot_send = jnp.sum(picked.astype(jnp.int32) * slot_each[:, None, :], axis=2)
    valid = jnp.any(picked, axis=2)
    code_store = delta_codes.reshape(slots, block_size, width)
    flat_slots = slot_send.reshape(-1)
    send_codes = code_store[flat_slots].reshape(holders, capacity, block_size, width)
    send_codes = jnp.where(valid[:, :, None, None], send_codes, jnp.zeros_like(send_codes))
    send_scales = delta_scales[flat_slots].reshape(holders, capacity, col_blocks)
    send_scales = jnp.where(valid[:, :, None], send_scales, jnp.zeros_like(send_scales))
    got_codes, got_scales = (
        lax.all_to_all(send_codes, "rep", split_axis=0, concat_axis=0, tiled=True),
        lax.all_to_all(send_scales, "rep", split_axis=0, concat_axis=0, tiled=True),
    )
    self_hot = (jnp.arange(holders, dtype=jnp.int32) == holder_self).astype(jnp.int32)
    source = jnp.sum(self_hot[:, None] * (holder_each * capacity + rank_each), axis=0)
    code_vals = got_codes.reshape(holders * capacity, block_size, width)[source].astype(jnp.float32)
    scale_vals = got_scales.reshape(holders * capacity, col_blocks)[source].astype(jnp.float32)
    scale_full = jnp.broadcast_to(
        scale_vals[:, None, :, None], (blocks, block_size, col_blocks, block_size)
    ).reshape(blocks, block_size, width)
    delta_full = (code_vals * scale_full).reshape(blocks * block_size, width)
    merged = (base_weight.astype(jnp.float32) + delta_full).astype(jnp.bfloat16)
    result = jnp.dot(
        lax.all_gather(tokens, "tp", axis=0, tiled=True), merged, preferred_element_type=jnp.float32
    )
    return result.astype(jnp.bfloat16)


def solution(mesh):
    in_specs = (
        P(("groups", "rep", "tp"), None),
        P(None, "tp"),
        P(("groups", "rep"), "tp"),
        P(("groups", "rep"), "tp"),
        P("groups"),
        P("groups", None),
    )
    out_specs = P(("groups", "rep"), "tp")
    return jax.shard_map(local, mesh=mesh, in_specs=in_specs, out_specs=out_specs, check_vma=False)
```

profile of v0, /device:TPU:0, one launch (start us, length us, event | category | flops | bytes accessed | tf_op | source)
XLA Modules:
  0.0 220.3 jit_solution(15624572698284385272)
XLA Ops:
  6.6 0.7 compare_convert_fusion.1
  7.2 0.8 multiply_reduce_fusion
  8.0 0.8 copy.13
  8.8 0.2 convert_reduce_fusion
  9.0 0.2 fusion.11
  9.2 0.2 select_reduce_fusion
  9.3 0.1 reshape.164
  9.4 0.7 gather_fusion.2
  10.1 0.1 copy.14
  10.2 0.6 broadcast_select_fusion.1
  10.8 4.2 %all-to-all-start.1 = ((bf16[4,24,4]{1,2,0:T(4,128)(2,1)}), bf16[4,24,4]{1,2,0:T(4,128)(2,1)S(1)}, u32[]{:S(2)}, u32[]{:S(2)}) async-start(bf16[4,24,4]{1,2,0:T(4,128)(2,1)} %broadcast_select_fusion.1), calls=%async_computation.1 | async-start | bytes 8192 | tf_op jit(solution)/shard_map/all_to_all | solution.py:40
  15.1 9.1 %gather_fusion = bf16[96,128,512]{2,1,0:T(8,128)(2,1)} fusion(bf16[32,128,512]{2,1,0:T(8,128)(2,1)} %bitcast.31, s32[1024]{0:T(1024)S(1)} %pad_clamp_fusion.1), kind=kCustom, calls=%fused_computation | custom fusion | bytes 25166208 | tf_op jit(solution)/shard_map/gather | solution.py:34
  24.1 10.7 %broadcast_select_fusion = bf16[4,24,128,512]{3,2,1,0:T(8,128)(2,1)} fusion(bf16[4,24,128,512]{3,2,1,0:T(8,128)(2,1)} %bitcast.30, pred[4,24]{1,0:T(4,128)(4,1)S(1)} %fusion.11), kind=kLoop, calls=%fused_computation.7 | loop fusion | flops 6291456 | bytes 25165920 | tf_op jit(solution)/shard_map/jit(_where)/select_n | solution.py:35
  34.8 0.0 all-to-all-done.1
  34.8 6.3 %all-to-all-start = ((bf16[4,24,128,512]{3,2,1,0:T(8,128)(2,1)}), bf16[4,24,128,512]{3,2,1,0:T(8,128)(2,1)}, u32[]{:S(2)}, u32[]{:S(2)}) async-start(bf16[4,24,128,512]{3,2,1,0:T(8,128)(2,1)} %broadcast_select_fusion), calls=%async_computation | async-start | bytes 25165824 | tf_op jit(solution)/shard_map/all_to_all | solution.py:39
  41.2 0.0 all-gather.2.cloned.1.call-start
  41.2 0.7 all-gather.2.cloned.1.call-update
  41.9 0.1 multiply_reduce_fusion.1
  42.0 0.1 copy.15
  42.1 0.6 gather_fusion.3
  42.8 136.5 %all-to-all-done = bf16[4,24,128,512]{3,2,1,0:T(8,128)(2,1)} async-done(((bf16[4,24,128,512]{3,2,1,0:T(8,128)(2,1)}), bf16[4,24,128,512]{3,2,1,0:T(8,128)(2,1)}, u32[]{:S(2)}, u32[]{:S(2)}) %all-to-all-start) | async-done | bytes 12582944 | tf_op jit(solution)/shard_map/all_to_all | solution.py:39
  179.3 10.1 %gather_fusion.1 = bf16[64,128,512]{2,1,0:T(8,128)(2,1)} fusion(bf16[96,128,512]{2,1,0:T(8,128)(2,1)} %bitcast.3, s32[1024]{0:T(1024)S(1)} %pad_clamp_fusion), kind=kCustom, calls=%fused_computation.1 | custom fusion | bytes 16777472 | tf_op jit(solution)/shard_map/gather | solution.py:44
  189.4 0.0 all-gather.2.cloned.1.call-done
  189.4 6.1 %broadcast_in_dim.23 = f32[64,128,4,128]{3,2,1,0:T(4,128)} broadcast(bf16[64,4]{1,0:T(8,128)(2,1)S(1)} %gather_fusion.3), dimensions={0,2} | broadcast | bytes 16777728 | tf_op jit(solution)/shard_map/broadcast_in_dim | solution.py:46
  195.4 17.1 %fusion.7 = bf16[384,512]{0,1:T(8,128)(2,1)S(1)} fusion(bf16[384,8192]{1,0:T(8,128)(2,1)} %all-gather.2.cloned.1.call-done, f32[1024,8,4,128]{3,2,1,0:T(4,128)} %bitcast.29, bf16[8192,512]{1,0:T(8,128)(2,1)} %bitcast.32, bf16[8192,512]{1,0:T(8,128)(2,1)} %param.7), kind=kOutput, calls=%fused_computation.10 | convolution fusion | flops 3242393600 | bytes 40239104 | tf_op jit(solution)/shard_map/dot_general | solution.py:51
  212.5 0.9 copy.16
  (8 shorter events, 0.1 us)
Async XLA Ops:
  10.8 24.0 %all-to-all-start.1 = ((bf16[4,24,4]{1,2,0:T(4,128)(2,1)}), bf16[4,24,4]{1,2,0:T(4,128)(2,1)S(1)}, u32[]{:S(2)}, u32[]{:S(2)}) async-start(bf16[4,24,4]{1,2,0:T(4,128)(2,1)} %broadcast_select_fusion.1), calls=%async_computation.1 | async-start | bytes 8192 | tf_op jit(solution)/shard_map/all_to_all | solution.py:40
  34.8 144.4 %all-to-all-start = ((bf16[4,24,128,512]{3,2,1,0:T(8,128)(2,1)}), bf16[4,24,128,512]{3,2,1,0:T(8,128)(2,1)}, u32[]{:S(2)}, u32[]{:S(2)}) async-start(bf16[4,24,128,512]{3,2,1,0:T(8,128)(2,1)} %broadcast_select_fusion), calls=%async_computation | async-start | bytes 25165824 | tf_op jit(solution)/shard_map/all_to_all | solution.py:39
  41.2 148.2 %all-gather.2.cloned.1.call-start = ((), (), s32[]{:S(2)}) async-start(), calls=%async_computation.2 | async-start | bytes 7864320 | tf_op jit(solution)/shard_map/all_gather | solution.py:52
Sparse Core Ops, SparseCore 0:
  43.6 117.5 all-gather.1
where the time goes:
time: 221 us; the launch traced here: 220 us
  waiting for transfers between devices  137 us (62%)
  local copies, waits for them, and re-layouts  28.6 us (13%)
  matrix products  17.1 us (8%)
  other arithmetic  13.4 us (6%)
  between operations  13.4 us (6%)
  starting transfers between devices  10.6 us (5%)
    all_to_all x1, waiting for transfers between devices, local(): lax.all_to_all(send_codes, 'rep', split_axis=0, concat_axis=0, tiled=True)  136 us
    dot_general x1, matrix products, local(): jnp.dot(lax.all_gather(tokens, 'tp', axis=0, tiled=True), merged, preferr...  17.1 us
    select_n x1, other arithmetic, local(): jnp.where(valid[:, :, None, None], send_codes, jnp.zeros_like(send_codes))  10.7 us
    gather x1, local copies, waits for them, and re-layouts, local(): got_codes.reshape(holders * capacity, block_size, width)[source]  10.1 us
    gather x1, local copies, waits for them, and re-layouts, local(): code_store[flat_slots].reshape(holders, capacity, block_size, width)  9.06 us
    all_to_all x1, starting transfers between devices, local(): lax.all_to_all(send_codes, 'rep', split_axis=0, concat_axis=0, tiled=True)  6.33 us
    broadcast_in_dim x1, local copies, waits for them, and re-layouts, local(): jnp.broadcast_to(scale_vals[:, None, :, None], (blocks, block_size, col_b...  6.05 us
  transfers between devices with their start and end apart: 3, of which 1 were waited for; matrix products, arithmetic and copies ran while one was open for 14% of the time, Pallas kernels for 0%

commit v1 on v0

v1 whole, which is shorter than its diff:
```python
import functools

import jax
import jax.numpy as jnp
from jax import lax
from jax.experimental import pallas as pl
from jax.experimental.pallas import tpu as pltpu
from jax.sharding import PartitionSpec as P

MESH = pl.DeviceIdType.MESH


def kernel(
    geo, variant_ref, home_ref, scale_ref, tok_ref, base_ref, code_ref, out_ref,
    tok_buf, code_buf, base_buf, scale_buf, scale_full, total,
    tok_send, tok_recv, code_send, code_recv, scale_send, scale_recv, local_sem,
):
    tps, reps, tok_parts, code_parts, slots, block, width = geo
    chips = reps // 2
    rep = lax.axis_index("rep")
    tp = lax.axis_index("tp")
    core = lax.rem(rep, 2)
    chip = rep // 2
    partner = {"rep": rep + 1 - 2 * core}
    depth = tok_ref.shape[1]
    tok_step = depth // tok_parts
    code_step = slots // code_parts

    own = [
        pltpu.make_async_copy(code_ref, code_buf.at[pl.ds(rep * slots, slots)], local_sem.at[0]),
        pltpu.make_async_copy(tok_ref, tok_buf.at[tp], local_sem.at[1]),
        pltpu.make_async_copy(base_ref, base_buf, local_sem.at[2]),
        pltpu.make_async_copy(scale_ref, scale_buf.at[rep], local_sem.at[3]),
    ]

    barrier = pltpu.get_barrier_semaphore()

    def greet(device):
        pl.semaphore_signal(barrier, inc=1, device_id=device, device_id_type=MESH)

    greet(partner)
    sides = []
    for axis, me, place, stride, count in (("tp", tp, tp, 1, tps), ("rep", rep, chip, 2, chips)):
        up = (place < count - 1, {axis: me + stride})
        down = (place > 0, {axis: me - stride})
        for there, device in (up, down):
            pl.when(there)(functools.partial(greet, device))
        sides.append((up, down))
    (tok_up, tok_down), (code_up, code_down) = sides
    met = 1 + sum(there.astype(jnp.int32) for there, _ in (tok_up, tok_down, code_up, code_down))
    pl.semaphore_wait(barrier, met)

    def tok_copy(src, owner, part, way, hop, device):
        cols = pl.ds(part * tok_step, tok_step)
        return pltpu.make_async_remote_copy(
            src_ref=tok_ref.at[:, cols] if src is None else tok_buf.at[owner, :, cols],
            dst_ref=tok_buf.at[owner, :, cols],
            send_sem=tok_send.at[way, hop, part],
            recv_sem=tok_recv.at[owner, part],
            device_id=device,
            device_id_type=MESH,
        )

    def code_copy(src, owner, part, way, hop, device):
        rows = pl.ds(owner * slots + part * code_step, code_step)
        return pltpu.make_async_remote_copy(
            src_ref=code_ref.at[pl.ds(part * code_step, code_step)] if src is None else code_buf.at[rows],
            dst_ref=code_buf.at[rows],
            send_sem=code_send.at[way, hop, part],
            recv_sem=code_recv.at[owner, part],
            device_id=device,
            device_id_type=MESH,
        )

    def scale_copy(src, owner, way, hop, device):
        return pltpu.make_async_remote_copy(
            src_ref=scale_ref if src is None else scale_buf.at[owner],
            dst_ref=scale_buf.at[owner],
            send_sem=scale_send.at[way, hop],
            recv_sem=scale_recv.at[owner],
            device_id=device,
            device_id_type=MESH,
        )

    for way, (there, device) in enumerate((code_up, code_down)):
        @pl.when(there)
        def _():
            scale_copy(None, rep, way, 0, device).start()
            for part in range(code_parts):
                code_copy(None, rep, part, way, 0, device).start()

    for way, (there, device) in enumerate((tok_up, tok_down)):
        @pl.when(there)
        def _():
            for part in range(tok_parts):
                tok_copy(None, tp, part, way, 0, device).start()

    scale_copy(None, rep, 2, 0, partner).start()
    for part in range(code_parts):
        code_copy(None, rep, part, 2, 0, partner).start()
    for copy in own:
        copy.start()

    events = [
        ((hop * tok_parts + part + 1) * tok_ref.shape[0] * tok_step, 0, hop, part)
        for hop in range(tps - 1) for part in range(tok_parts)
    ] + [
        ((hop * code_parts + part + 1) * code_step * block * width, 1, hop, part)
        for hop in range(chips - 1) for part in range(code_parts)
    ]
    for _, kind, hop, part in sorted(events):
        for way in range(2):
            sign = 1 - 2 * way
            if kind == 0:
                place, count = tp, tps
                origin = tp - sign * (hop + 1)
                owner = origin
                onward = (tok_up, tok_down)[way]
            else:
                place, count = chip, chips
                origin = chip - sign * (hop + 1)
                owner = rep - 2 * sign * (hop + 1)
                onward = (code_up, code_down)[way]

            @pl.when((origin >= 0) & (origin < count))
            def _():
                if kind == 0:
                    tok_copy(1, owner, part, way, 0, partner).wait_recv()
                    if hop < tps - 2:
                        @pl.when(onward[0])
                        def _():
                            tok_copy(1, owner, part, way, hop + 1, onward[1]).start()
                else:
                    if part == 0:
                        scale_copy(1, owner, way, 0, partner).wait_recv()
                    code_copy(1, owner, part, way, 0, partner).wait_recv()
                    if part == 0:
                        scale_copy(1, owner, 2 + way, hop + 1, partner).start()
                    code_copy(1, owner, part, 2 + way, hop + 1, partner).start()
                    if hop < chips - 2:
                        @pl.when(onward[0])
                        def _():
                            if part == 0:
                                scale_copy(1, owner, way, hop + 1, onward[1]).start()
                            code_copy(1, owner, part, way, hop + 1, onward[1]).start()

    for other in range(chips):
        owner = 2 * other + 1 - core
        scale_copy(1, owner, 0, 0, partner).wait_recv()
        for part in range(code_parts):
            code_copy(1, owner, part, 0, 0, partner).wait_recv()
    for copy in own:
        copy.wait()

    for owner in range(reps):
        scales = scale_buf[owner].astype(jnp.float32)
        for col in range(scales.shape[1]):
            scale_full[owner * slots:(owner + 1) * slots, col * block:(col + 1) * block] = (
                jnp.broadcast_to(scales[:, col:col + 1], (slots, block))
            )

    variant = variant_ref[rep]
    group = 4
    total[...] = jnp.zeros_like(total)

    def multiply(step, carry):
        merged = []
        for i in range(group):
            b = step * group + i
            e = home_ref[variant, b]
            delta = code_buf[e].astype(jnp.float32) * scale_full[pl.ds(e, 1), :]
            rows = pl.ds(pl.multiple_of(b * block, block), block)
            merged.append((base_buf[rows, :].astype(jnp.float32) + delta).astype(jnp.bfloat16))
        span = group * block
        cols = pl.ds(pl.multiple_of(step * span, span), span)
        prompt = tok_buf[:, :, cols].reshape(total.shape[0], span)
        total[...] += jnp.dot(prompt, jnp.concatenate(merged, axis=0), preferred_element_type=jnp.float32)
        return carry

    lax.fori_loop(0, depth // (group * block), multiply, 0)
    out_ref[...] = total[...].astype(out_ref.dtype)

    for way, (there, device) in enumerate((tok_up, tok_down)):
        for hop in range(tps - 1):
            origin = tp - (1 - 2 * way) * hop

            @pl.when(there & (origin >= 0) & (origin < tps))
            def _():
                for part in range(tok_parts):
                    tok_copy(1, origin, part, way, hop, device).wait_send()
    for way, (there, device) in enumerate((code_up, code_down)):
        sign = 1 - 2 * way
        for hop in range(chips):
            origin = chip - sign * hop
            owner = rep - 2 * sign * hop
            here = (origin >= 0) & (origin < chips)
            if hop < chips - 1:
                @pl.when(there & here)
                def _():
                    scale_copy(1, owner, way, hop, device).wait_send()
                    for part in range(code_parts):
                        code_copy(1, owner, part, way, hop, device).wait_send()
            if hop or not way:
                @pl.when(here)
                def _():
                    scale_copy(1, owner, 2 + way, hop, partner).wait_send()
                    for part in range(code_parts):
                        code_copy(1, owner, part, 2 + way, hop, partner).wait_send()


def local(tps, reps, tokens, base_weight, delta_codes, delta_scales, replica_variant, block_home):
    slots, col_blocks = delta_scales.shape
    rows, depth = tokens.shape
    width = base_weight.shape[1]
    block = delta_codes.shape[0] // slots
    tok_parts = max(1, 16 // tps)
    code_parts = max(1, 32 // reps)
    codes = delta_codes.reshape(slots, block, width)
    dma = pltpu.SemaphoreType.DMA
    chips = reps // 2
    return pl.pallas_call(
        functools.partial(kernel, (tps, reps, tok_parts, code_parts, slots, block, width)),
        out_shape=jax.ShapeDtypeStruct((tps * rows, width), jnp.bfloat16),
        in_specs=[pl.BlockSpec(memory_space=pltpu.SMEM)] * 2
        + [pl.BlockSpec(memory_space=pltpu.VMEM)]
        + [pl.BlockSpec(memory_space=pl.ANY)] * 3,
        out_specs=pl.BlockSpec(memory_space=pltpu.VMEM),
        scratch_shapes=[
            pltpu.VMEM((tps, rows, depth), jnp.bfloat16),
            pltpu.VMEM((reps * slots, block, width), jnp.bfloat16),
            pltpu.VMEM((depth, width), jnp.bfloat16),
            pltpu.VMEM((reps, slots, col_blocks), jnp.bfloat16),
            pltpu.VMEM((reps * slots, width), jnp.float32),
            pltpu.VMEM((tps * rows, width), jnp.float32),
            dma((2, tps, tok_parts)),
            dma((tps, tok_parts)),
            dma((4, chips, code_parts)),
            dma((reps, code_parts)),
            dma((4, chips)),
            dma((reps,)),
            dma((4,)),
        ],
        compiler_params=pltpu.CompilerParams(
            collective_id=0, has_side_effects=True, vmem_limit_bytes=60 * 1024 * 1024
        ),
    )(replica_variant, block_home, delta_scales, tokens, base_weight, codes)


def solution(mesh):
    in_specs = (
        P(("groups", "rep", "tp"), None),
        P(None, "tp"),
        P(("groups", "rep"), "tp"),
        P(("groups", "rep"), "tp"),
        P("groups"),
        P("groups", None),
    )
    out_specs = P(("groups", "rep"), "tp")
    body = functools.partial(local, mesh.shape["tp"], mesh.shape["rep"])
    return jax.shard_map(body, mesh=mesh, in_specs=in_specs, out_specs=out_specs, check_vma=False)
```

time: 221 us -> 120 us (0.54)
  waiting for transfers between devices: 137 us -> 0 us
  Pallas kernels: 0 us -> 116 us
  local copies, waits for them, and re-layouts: 28.6 us -> 3.13 us
  matrix products: 17.1 us -> 0 us
  other arithmetic: 13.4 us -> 0 us
  between operations: 13.4 us -> 0.01 us
  starting transfers between devices: 10.6 us -> 0 us
    all_to_all x2 -> x0, waiting for transfers between devices: 136 us -> none  [the longest x1 136 us: local(): lax.all_to_all(send_codes, 'rep', split_axis=0, concat_axis=0, tiled=True)]
    pallas_call x0 -> x1, Pallas kernels: none -> 116 us  [local(): pl.pallas_call(functools.partial(kernel, (tps, reps, tok_parts, code_part...]
    gather x4 -> x0, local copies, waits for them, and re-layouts: 20.5 us -> none  [the longest x1 10.1 us: local(): got_codes.reshape(holders * capacity, block_size, width)[source]]
    dot_general x1 -> x0, matrix products: 17.1 us -> none  [local(): jnp.dot(lax.all_gather(tokens, 'tp', axis=0, tiled=True), merged, preferr...]
    select_n x5 -> x0, other arithmetic: 11.3 us -> none  [the longest x1 10.7 us: local(): jnp.where(valid[:, :, None, None], send_codes, jnp.zeros_like(send_codes))]
    all_to_all x2 -> x0, starting transfers between devices: 10.6 us -> none  [the longest x1 6.33 us: local(): lax.all_to_all(send_codes, 'rep', split_axis=0, concat_axis=0, tiled=True)]
    broadcast_in_dim x1 -> x0, local copies, waits for them, and re-layouts: 6.05 us -> none  [local(): jnp.broadcast_to(scale_vals[:, None, :, None], (blocks, block_size, col_b...]
    unnamed x1 -> x2, local copies, waits for them, and re-layouts: 0.78 us -> 3.13 us
  transfers between devices with their start and end apart: 3 -> 0, of which waited for: 1 -> 0; matrix products, arithmetic and copies ran while one was open for 14% -> 0% of each run, Pallas kernels for 0% -> 0%
where the time goes in v1:
time: 120 us
  Pallas kernels  116 us (97%)
  local copies, waits for them, and re-layouts  3.13 us (3%)
    pallas_call x1, Pallas kernels, local(): pl.pallas_call(functools.partial(kernel, (tps, reps, tok_parts, code_part...  116 us
    unnamed x2, local copies, waits for them, and re-layouts  3.13 us

profile of v1, /device:TPU:0, one launch (start us, length us, event | category | flops | bytes accessed | tf_op | source)
XLA Modules:
  0.0 119.6 jit_solution(13628944064422152978)
XLA Ops:
  0.0 1.4 %copy.7.scale_ref = bf16[32,4]{1,0:T(8,128)(2,1)} copy(bf16[32,4]{0,1:T(4,128)(2,1)} %param.9) | data formatting | bytes 512 | tf_op args[3]
  1.4 116.4 %shard_map.64 = bf16[384,512]{1,0:T(8,128)(2,1)} custom-call(s32[4]{0:T(128)} %variant_ref.1, s32[2,64]{1,0:T(2,128)} %home_ref.1, bf16[32,4]{1,0:T(8,128)(2,1)} %copy.7.scale_ref, bf16[96,8192]{1,0:T(8,128)(2,1)} %tok_ref.1, bf16[8192,512]{1,0:T(8,128)(2,1)} %base_ref.1, bf16[32,128,512]{2,1,0:T(8,128)(2,1)} %bitcast.1), custom_call_target="tpu_custom_call" | custom-call | tf_op jit(solution)/shard_map/pallas_call | solution.py:221
  117.8 1.8 %copy.9 = bf16[384,512]{1,0:T(8,128)(2,1)} copy(bf16[384,512]{1,0:T(8,128)(2,1)} %shard_map.64) | data formatting | bytes 786432

commit v2 on v1

--- a/solution.py
+++ b/solution.py
@@ -82,6 +82,12 @@
             device_id_type=MESH,
         )
 
+    for way, (there, device) in enumerate((tok_up, tok_down)):
+        @pl.when(there)
+        def _():
+            for part in range(tok_parts):
+                tok_copy(None, tp, part, way, 0, device).start()
+
     for way, (there, device) in enumerate((code_up, code_down)):
         @pl.when(there)
         def _():
@@ -89,12 +95,6 @@
             for part in range(code_parts):
                 code_copy(None, rep, part, way, 0, device).start()
 
-    for way, (there, device) in enumerate((tok_up, tok_down)):
-        @pl.when(there)
-        def _():
-            for part in range(tok_parts):
-                tok_copy(None, tp, part, way, 0, device).start()
-
     scale_copy(None, rep, 2, 0, partner).start()
     for part in range(code_parts):
         code_copy(None, rep, part, 2, 0, partner).start()
@@ -103,7 +103,7 @@
 
     events = [
         ((hop * tok_parts + part + 1) * tok_ref.shape[0] * tok_step, 0, hop, part)
-        for hop in range(tps - 1) for part in range(tok_parts)
+        for hop in range(tps - 2) for part in range(tok_parts)
     ] + [
         ((hop * code_parts + part + 1) * code_step * block * width, 1, hop, part)
         for hop in range(chips - 1) for part in range(code_parts)
@@ -126,10 +126,9 @@
             def _():
                 if kind == 0:
                     tok_copy(1, owner, part, way, 0, partner).wait_recv()
-                    if hop < tps - 2:
-                        @pl.when(onward[0])
-                        def _():
-                            tok_copy(1, owner, part, way, hop + 1, onward[1]).start()
+                    @pl.when(onward[0])
+                    def _():
+                        tok_copy(1, owner, part, way, hop + 1, onward[1]).start()
                 else:
                     if part == 0:
                         scale_copy(1, owner, way, 0, partner).wait_recv()
@@ -152,33 +151,67 @@
     for copy in own:
         copy.wait()
 
+    slot_row = lax.broadcasted_iota(jnp.int32, (slots, slots), 0)
+    diagonal = slot_row == lax.broadcasted_iota(jnp.int32, (slots, slots), 1)
     for owner in range(reps):
         scales = scale_buf[owner].astype(jnp.float32)
-        for col in range(scales.shape[1]):
+        for col in range(scales.shape[0]):
+            across = jnp.broadcast_to(scales[col:col + 1, :], (slots, slots))
+            down = jnp.sum(jnp.where(diagonal, across, 0.0), axis=1, keepdims=True)
             scale_full[owner * slots:(owner + 1) * slots, col * block:(col + 1) * block] = (
-                jnp.broadcast_to(scales[:, col:col + 1], (slots, block))
+                jnp.broadcast_to(down, (slots, block))
             )
 
     variant = variant_ref[rep]
+    rows = tok_ref.shape[0]
     group = 4
-    total[...] = jnp.zeros_like(total)
-
-    def multiply(step, carry):
-        merged = []
-        for i in range(group):
-            b = step * group + i
-            e = home_ref[variant, b]
-            delta = code_buf[e].astype(jnp.float32) * scale_full[pl.ds(e, 1), :]
-            rows = pl.ds(pl.multiple_of(b * block, block), block)
-            merged.append((base_buf[rows, :].astype(jnp.float32) + delta).astype(jnp.bfloat16))
-        span = group * block
-        cols = pl.ds(pl.multiple_of(step * span, span), span)
-        prompt = tok_buf[:, :, cols].reshape(total.shape[0], span)
-        total[...] += jnp.dot(prompt, jnp.concatenate(merged, axis=0), preferred_element_type=jnp.float32)
-        return carry
-
-    lax.fori_loop(0, depth // (group * block), multiply, 0)
-    out_ref[...] = total[...].astype(out_ref.dtype)
+    span = group * block
+
+    def merge_and_multiply(first, shards):
+        here = pl.ds(0, shards * rows)
+        total[here, :] = jnp.zeros((shards * rows, width), jnp.float32)
+
+        def step(at, carry):
+            merged = []
+            for i in range(group):
+                b = at * group + i
+                e = home_ref[variant, b]
+                delta = code_buf[e].astype(jnp.float32) * scale_full[pl.ds(e, 1), :]
+                lines = pl.ds(pl.multiple_of(b * block, block), block)
+                merged.append((base_buf[lines, :].astype(jnp.float32) + delta).astype(jnp.bfloat16))
+            merged = jnp.concatenate(merged, axis=0)
+            cols = pl.ds(pl.multiple_of(at * span, span), span)
+            if shards < tps:
+                base_buf[cols, :] = merged
+            prompt = tok_buf[pl.ds(first, shards), :, cols].reshape(shards * rows, span)
+            total[here, :] += jnp.dot(prompt, merged, preferred_element_type=jnp.float32)
+            return carry
+
+        lax.fori_loop(0, depth // span, step, 0)
+        out_ref[pl.ds(pl.multiple_of(first * rows, rows), shards * rows), :] = total[here, :].astype(out_ref.dtype)
+
+    at_end = (tp == 0) | (tp == tps - 1)
+
+    @pl.when(at_end)
+    def _():
+        merge_and_multiply((tp > 0).astype(jnp.int32), tps - 1)
+        far = tps - 1 - tp
+        last = pl.ds(0, rows)
+        total[last, :] = jnp.zeros((rows, width), jnp.float32)
+        for part in range(tok_parts):
+            tok_copy(1, far, part, 0, 0, partner).wait_recv()
+
+            def step(at, carry):
+                cols = pl.ds(pl.multiple_of(part * tok_step + at * span, span), span)
+                total[last, :] += jnp.dot(tok_buf[far, :, cols], base_buf[cols, :], preferred_element_type=jnp.float32)
+                return carry
+
+            lax.fori_loop(0, tok_step // span, step, 0)
+        out_ref[pl.ds(pl.multiple_of(far * rows, rows), rows), :] = total[last, :].astype(out_ref.dtype)
+
+    @pl.when(jnp.logical_not(at_end))
+    def _():
+        merge_and_multiply(0, tps)
 
     for way, (there, device) in enumerate((tok_up, tok_down)):
         for hop in range(tps - 1):
@@ -213,7 +246,7 @@
     rows, depth = tokens.shape
     width = base_weight.shape[1]
     block = delta_codes.shape[0] // slots
-    tok_parts = max(1, 16 // tps)
+    tok_parts = max(1, 32 // tps)
     code_parts = max(1, 32 // reps)
     codes = delta_codes.reshape(slots, block, width)
     dma = pltpu.SemaphoreType.DMA
@@ -222,14 +255,13 @@
         functools.partial(kernel, (tps, reps, tok_parts, code_parts, slots, block, width)),
         out_shape=jax.ShapeDtypeStruct((tps * rows, width), jnp.bfloat16),
         in_specs=[pl.BlockSpec(memory_space=pltpu.SMEM)] * 2
-        + [pl.BlockSpec(memory_space=pltpu.VMEM)]
-        + [pl.BlockSpec(memory_space=pl.ANY)] * 3,
+        + [pl.BlockSpec(memory_space=pl.ANY)] * 4,
         out_specs=pl.BlockSpec(memory_space=pltpu.VMEM),
         scratch_shapes=[
             pltpu.VMEM((tps, rows, depth), jnp.bfloat16),
             pltpu.VMEM((reps * slots, block, width), jnp.bfloat16),
             pltpu.VMEM((depth, width), jnp.bfloat16),
-            pltpu.VMEM((reps, slots, col_blocks), jnp.bfloat16),
+            pltpu.VMEM((reps, col_blocks, slots), jnp.bfloat16),
             pltpu.VMEM((reps * slots, width), jnp.float32),
             pltpu.VMEM((tps * rows, width), jnp.float32),
             dma((2, tps, tok_parts)),
@@ -243,7 +275,7 @@
         compiler_params=pltpu.CompilerParams(
             collective_id=0, has_side_effects=True, vmem_limit_bytes=60 * 1024 * 1024
         ),
-    )(replica_variant, block_home, delta_scales, tokens, base_weight, codes)
+    )(replica_variant, block_home, delta_scales.T, tokens, base_weight, codes)
 
 
 def solution(mesh):

time: 120 us -> 113 us (0.942)
  Pallas kernels: 116 us -> 110 us
  local copies, waits for them, and re-layouts: 3.13 us -> 1.77 us
    pallas_call x1, Pallas kernels: 116 us -> 110 us  [local(): pl.pallas_call(functools.partial(kernel, (tps, reps, tok_parts, code_part...]
    unnamed x2 -> x1, local copies, waits for them, and re-layouts: 3.13 us -> 1.77 us
where the time goes in v2:
time: 113 us; the launch traced here: 112 us
  Pallas kernels  110 us (97%)
  local copies, waits for them, and re-layouts  1.77 us (2%)
    pallas_call x1, Pallas kernels, local(): pl.pallas_call(functools.partial(kernel, (tps, reps, tok_parts, code_part...  110 us

profile of v2, /device:TPU:0, one launch (start us, length us, event | category | flops | bytes accessed | tf_op | source)
XLA Modules:
  0.0 112.1 jit_solution(11221949406700226041)
XLA Ops:
  0.0 110.3 %shard_map.64 = bf16[384,512]{1,0:T(8,128)(2,1)} custom-call(s32[4]{0:T(128)} %variant_ref.1, s32[2,64]{1,0:T(2,128)} %home_ref.1, bf16[4,32]{1,0:T(4,128)(2,1)} %bitcast.3, bf16[96,8192]{1,0:T(8,128)(2,1)} %tok_ref.1, bf16[8192,512]{1,0:T(8,128)(2,1)} %base_ref.1, bf16[32,128,512]{2,1,0:T(8,128)(2,1)} %bitcast.2), custom_call_target="tpu_custom_call" | custom-call | tf_op jit(solution)/shard_map/pallas_call | solution.py:254
  110.3 1.8 %copy.8 = bf16[384,512]{1,0:T(8,128)(2,1)} copy(bf16[384,512]{1,0:T(8,128)(2,1)} %shard_map.64) | data formatting | bytes 786432

commit v3 on v2

--- a/solution.py
+++ b/solution.py
@@ -11,8 +11,8 @@
 
 
 def kernel(
-    geo, variant_ref, home_ref, scale_ref, tok_ref, base_ref, code_ref, out_ref,
-    tok_buf, code_buf, base_buf, scale_buf, scale_full, total,
+    geo, variants_ref, homes_ref, scale_ref, tok_ref, base_ref, code_ref, out_ref,
+    variant_ref, home_ref, tok_buf, code_buf, base_buf, scale_buf, scale_full, total,
     tok_send, tok_recv, code_send, code_recv, scale_send, scale_recv, local_sem,
 ):
     tps, reps, tok_parts, code_parts, slots, block, width = geo
@@ -23,7 +23,6 @@
     chip = rep // 2
     partner = {"rep": rep + 1 - 2 * core}
     depth = tok_ref.shape[1]
-    tok_step = depth // tok_parts
     code_step = slots // code_parts
 
     own = [
@@ -31,6 +30,8 @@
         pltpu.make_async_copy(tok_ref, tok_buf.at[tp], local_sem.at[1]),
         pltpu.make_async_copy(base_ref, base_buf, local_sem.at[2]),
         pltpu.make_async_copy(scale_ref, scale_buf.at[rep], local_sem.at[3]),
+        pltpu.make_async_copy(variants_ref, variant_ref, local_sem.at[4]),
+        pltpu.make_async_copy(homes_ref, home_ref, local_sem.at[5]),
     ]
 
     barrier = pltpu.get_barrier_semaphore()
@@ -51,7 +52,7 @@
     pl.semaphore_wait(barrier, met)
 
     def tok_copy(src, owner, part, way, hop, device):
-        cols = pl.ds(part * tok_step, tok_step)
+        cols = pl.ds(*tok_parts[part])
         return pltpu.make_async_remote_copy(
             src_ref=tok_ref.at[:, cols] if src is None else tok_buf.at[owner, :, cols],
             dst_ref=tok_buf.at[owner, :, cols],
@@ -85,7 +86,7 @@
     for way, (there, device) in enumerate((tok_up, tok_down)):
         @pl.when(there)
         def _():
-            for part in range(tok_parts):
+            for part in range(len(tok_parts)):
                 tok_copy(None, tp, part, way, 0, device).start()
 
     for way, (there, device) in enumerate((code_up, code_down)):
@@ -102,8 +103,8 @@
         copy.start()
 
     events = [
-        ((hop * tok_parts + part + 1) * tok_ref.shape[0] * tok_step, 0, hop, part)
-        for hop in range(tps - 2) for part in range(tok_parts)
+        ((hop * depth + sum(tok_parts[part])) * tok_ref.shape[0], 0, hop, part)
+        for hop in range(tps - 2) for part in range(len(tok_parts))
     ] + [
         ((hop * code_parts + part + 1) * code_step * block * width, 1, hop, part)
         for hop in range(chips - 1) for part in range(code_parts)
@@ -198,15 +199,15 @@
         far = tps - 1 - tp
         last = pl.ds(0, rows)
         total[last, :] = jnp.zeros((rows, width), jnp.float32)
-        for part in range(tok_parts):
+        for part in range(len(tok_parts)):
             tok_copy(1, far, part, 0, 0, partner).wait_recv()
 
             def step(at, carry):
-                cols = pl.ds(pl.multiple_of(part * tok_step + at * span, span), span)
+                cols = pl.ds(pl.multiple_of(tok_parts[part][0] + at * span, span), span)
                 total[last, :] += jnp.dot(tok_buf[far, :, cols], base_buf[cols, :], preferred_element_type=jnp.float32)
                 return carry
 
-            lax.fori_loop(0, tok_step // span, step, 0)
+            lax.fori_loop(0, tok_parts[part][1] // span, step, 0)
         out_ref[pl.ds(pl.multiple_of(far * rows, rows), rows), :] = total[last, :].astype(out_ref.dtype)
 
     @pl.when(jnp.logical_not(at_end))
@@ -219,7 +220,7 @@
 
             @pl.when(there & (origin >= 0) & (origin < tps))
             def _():
-                for part in range(tok_parts):
+                for part in range(len(tok_parts)):
                     tok_copy(1, origin, part, way, hop, device).wait_send()
     for way, (there, device) in enumerate((code_up, code_down)):
         sign = 1 - 2 * way
@@ -246,7 +247,8 @@
     rows, depth = tokens.shape
     width = base_weight.shape[1]
     block = delta_codes.shape[0] // slots
-    tok_parts = max(1, 32 // tps)
+    sizes = (depth // 2, depth // 4, depth // 8, depth // 8)
+    tok_parts = tuple((sum(sizes[:i]), size) for i, size in enumerate(sizes))
     code_parts = max(1, 32 // reps)
     codes = delta_codes.reshape(slots, block, width)
     dma = pltpu.SemaphoreType.DMA
@@ -254,23 +256,24 @@
     return pl.pallas_call(
         functools.partial(kernel, (tps, reps, tok_parts, code_parts, slots, block, width)),
         out_shape=jax.ShapeDtypeStruct((tps * rows, width), jnp.bfloat16),
-        in_specs=[pl.BlockSpec(memory_space=pltpu.SMEM)] * 2
-        + [pl.BlockSpec(memory_space=pl.ANY)] * 4,
+        in_specs=[pl.BlockSpec(memory_space=pl.ANY)] * 6,
         out_specs=pl.BlockSpec(memory_space=pltpu.VMEM),
         scratch_shapes=[
+            pltpu.SMEM(replica_variant.shape, jnp.int32),
+            pltpu.SMEM(block_home.shape, jnp.int32),
             pltpu.VMEM((tps, rows, depth), jnp.bfloat16),
             pltpu.VMEM((reps * slots, block, width), jnp.bfloat16),
             pltpu.VMEM((depth, width), jnp.bfloat16),
             pltpu.VMEM((reps, col_blocks, slots), jnp.bfloat16),
             pltpu.VMEM((reps * slots, width), jnp.float32),
             pltpu.VMEM((tps * rows, width), jnp.float32),
-            dma((2, tps, tok_parts)),
-            dma((tps, tok_parts)),
+            dma((2, tps, len(tok_parts))),
+            dma((tps, len(tok_parts))),
             dma((4, chips, code_parts)),
             dma((reps, code_parts)),
             dma((4, chips)),
             dma((reps,)),
-            dma((4,)),
+            dma((6,)),
         ],
         compiler_params=pltpu.CompilerParams(
             collective_id=0, has_side_effects=True, vmem_limit_bytes=60 * 1024 * 1024

time: 113 us -> 111 us (0.982)
    pallas_call x1, Pallas kernels: 110 us -> 109 us  [local(): pl.pallas_call(functools.partial(kernel, (tps, reps, tok_parts, code_part...]
where the time goes in v3:
time: 111 us
  Pallas kernels  109 us (98%)
  local copies, waits for them, and re-layouts  1.77 us (2%)
    pallas_call x1, Pallas kernels, local(): pl.pallas_call(functools.partial(kernel, (tps, reps, tok_parts, code_part...  109 us

profile of v3, /device:TPU:0, one launch (start us, length us, event | category | flops | bytes accessed | tf_op | source)
XLA Modules:
  0.0 110.9 jit_solution(9410862007325526488)
XLA Ops:
  0.0 109.1 %shard_map.64 = bf16[384,512]{1,0:T(8,128)(2,1)} custom-call(s32[4]{0:T(128)} %variants_ref.1, s32[2,64]{1,0:T(2,128)} %homes_ref.1, bf16[4,32]{1,0:T(4,128)(2,1)} %bitcast.3, bf16[96,8192]{1,0:T(8,128)(2,1)} %tok_ref.1, bf16[8192,512]{1,0:T(8,128)(2,1)} %base_ref.1, bf16[32,128,512]{2,1,0:T(8,128)(2,1)} %bitcast.2), custom_call_target="tpu_custom_call" | custom-call | tf_op jit(solution)/shard_map/pallas_call | solution.py:256
  109.1 1.8 %copy.8 = bf16[384,512]{1,0:T(8,128)(2,1)} copy(bf16[384,512]{1,0:T(8,128)(2,1)} %shard_map.64) | data formatting | bytes 786432

commit v4 on v3

--- a/solution.py
+++ b/solution.py
@@ -165,7 +165,7 @@
 
     variant = variant_ref[rep]
     rows = tok_ref.shape[0]
-    group = 4
+    group = 8
     span = group * block
 
     def merge_and_multiply(first, shards):
@@ -251,6 +251,10 @@
     tok_parts = tuple((sum(sizes[:i]), size) for i, size in enumerate(sizes))
     code_parts = max(1, 32 // reps)
     codes = delta_codes.reshape(slots, block, width)
+    operands = [
+        pltpu.with_memory_space_constraint(x, pltpu.HBM)
+        for x in (replica_variant, block_home, delta_scales.T, tokens, base_weight, codes)
+    ]
     dma = pltpu.SemaphoreType.DMA
     chips = reps // 2
     return pl.pallas_call(
@@ -276,9 +280,9 @@
             dma((6,)),
         ],
         compiler_params=pltpu.CompilerParams(
-            collective_id=0, has_side_effects=True, vmem_limit_bytes=60 * 1024 * 1024
+            collective_id=0, has_side_effects=True, vmem_limit_bytes=54 * 1024 * 1024
         ),
-    )(replica_variant, block_home, delta_scales.T, tokens, base_weight, codes)
+    )(*operands)
 
 
 def solution(mesh):

time: 111 us -> 111 us (level)
  no operation moved by 1% of the time
where the time goes in v4:
time: 111 us
  Pallas kernels  109 us (98%)
  local copies, waits for them, and re-layouts  1.77 us (2%)
    pallas_call x1, Pallas kernels, local(): pl.pallas_call(functools.partial(kernel, (tps, reps, tok_parts, code_part...  109 us

profile of v4, /device:TPU:0, one launch (start us, length us, event | category | flops | bytes accessed | tf_op | source)
XLA Modules:
  0.0 110.8 jit_solution(4454135804774191810)
XLA Ops:
  0.0 109.0 %shard_map.64 = bf16[384,512]{1,0:T(8,128)(2,1)} custom-call(s32[4]{0:T(128)} %variants_ref.1, s32[2,64]{1,0:T(2,128)} %homes_ref.1, bf16[4,32]{1,0:T(4,128)(2,1)} %bitcast.3, bf16[96,8192]{1,0:T(8,128)(2,1)} %tok_ref.1, bf16[8192,512]{1,0:T(8,128)(2,1)} %base_ref.1, bf16[32,128,512]{2,1,0:T(8,128)(2,1)} %bitcast.2), custom_call_target="tpu_custom_call" | custom-call | tf_op jit(solution)/shard_map/pallas_call | solution.py:260
  109.0 1.8 %copy.8 = bf16[384,512]{1,0:T(8,128)(2,1)} copy(bf16[384,512]{1,0:T(8,128)(2,1)} %shard_map.64) | data formatting | bytes 786432

commit v5 on v4

--- a/solution.py
+++ b/solution.py
@@ -249,7 +249,7 @@
     block = delta_codes.shape[0] // slots
     sizes = (depth // 2, depth // 4, depth // 8, depth // 8)
     tok_parts = tuple((sum(sizes[:i]), size) for i, size in enumerate(sizes))
-    code_parts = max(1, 32 // reps)
+    code_parts = max(1, 8 // reps)
     codes = delta_codes.reshape(slots, block, width)
     operands = [
         pltpu.with_memory_space_constraint(x, pltpu.HBM)
@@ -280,7 +280,7 @@
             dma((6,)),
         ],
         compiler_params=pltpu.CompilerParams(
-            collective_id=0, has_side_effects=True, vmem_limit_bytes=54 * 1024 * 1024
+            collective_id=0, has_side_effects=True, vmem_limit_bytes=48 * 1024 * 1024
         ),
     )(*operands)
 

time: 111 us -> 108 us (0.973)
    pallas_call x1, Pallas kernels: 109 us -> 108 us  [local(): pl.pallas_call(functools.partial(kernel, (tps, reps, tok_parts, code_part...]
where the time goes in v5:
time: 108 us
  Pallas kernels  108 us (100%)
    pallas_call x1, Pallas kernels, local(): pl.pallas_call(functools.partial(kernel, (tps, reps, tok_parts, code_part...  108 us

profile of v5, /device:TPU:0, one launch (start us, length us, event | category | flops | bytes accessed | tf_op | source)
XLA Modules:
  0.0 108.3 jit_solution(17200481634057425396)
XLA Ops:
  0.0 107.6 %shard_map.64 = bf16[384,512]{1,0:T(8,128)(2,1)S(1)} custom-call(s32[4]{0:T(128)} %variants_ref.1, s32[2,64]{1,0:T(2,128)} %homes_ref.1, bf16[4,32]{1,0:T(4,128)(2,1)} %bitcast.3, bf16[96,8192]{1,0:T(8,128)(2,1)} %tok_ref.1, bf16[8192,512]{1,0:T(8,128)(2,1)} %base_ref.1, bf16[32,128,512]{2,1,0:T(8,128)(2,1)} %bitcast.2), custom_call_target="tpu_custom_call" | custom-call | tf_op jit(solution)/shard_map/pallas_call | solution.py:260
  107.6 0.7 copy.8

commit v6 on v5

--- a/solution.py
+++ b/solution.py
@@ -247,7 +247,7 @@
     rows, depth = tokens.shape
     width = base_weight.shape[1]
     block = delta_codes.shape[0] // slots
-    sizes = (depth // 2, depth // 4, depth // 8, depth // 8)
+    sizes = (depth // 2, 3 * depth // 8, depth // 8)
     tok_parts = tuple((sum(sizes[:i]), size) for i, size in enumerate(sizes))
     code_parts = max(1, 8 // reps)
     codes = delta_codes.reshape(slots, block, width)

time: 108 us -> 108 us (level)
  no operation moved by 1% of the time
where the time goes in v6:
time: 108 us
  Pallas kernels  107 us (99%)
    pallas_call x1, Pallas kernels, local(): pl.pallas_call(functools.partial(kernel, (tps, reps, tok_parts, code_part...  107 us

profile of v6, /device:TPU:0, one launch (start us, length us, event | category | flops | bytes accessed | tf_op | source)
XLA Modules:
  0.0 108.2 jit_solution(9039405874700140495)
XLA Ops:
  0.0 107.4 %shard_map.64 = bf16[384,512]{1,0:T(8,128)(2,1)S(1)} custom-call(s32[4]{0:T(128)} %variants_ref.1, s32[2,64]{1,0:T(2,128)} %homes_ref.1, bf16[4,32]{1,0:T(4,128)(2,1)} %bitcast.3, bf16[96,8192]{1,0:T(8,128)(2,1)} %tok_ref.1, bf16[8192,512]{1,0:T(8,128)(2,1)} %base_ref.1, bf16[32,128,512]{2,1,0:T(8,128)(2,1)} %bitcast.2), custom_call_target="tpu_custom_call" | custom-call | tf_op jit(solution)/shard_map/pallas_call | solution.py:260
  107.5 0.7 copy.8
